TPU v7x, 32 devices: a whole 2x2x4 slice. The times are simulated.
32 devices in a mesh: rep: 4 (over x, core), shard: 8 (over z, y).
Axes of the slice: x: 2, y: 2, z: 4, core: 2. Of those that a mesh axis runs over, the one named last changes fastest.
Arguments:
- tokens: bfloat16 [4096, 2048], P(('rep', 'shard')), may hold values from -6 to 6
- segment_ids: int32 [4096], P(('rep', 'shard')), may hold values from 0 to 15, as said below
- positions: int32 [4096], P(('rep', 'shard')), may hold values from 0 to 127, as said below
- first_gain: float32 [2048], P('shard'), may hold values from 0.1 to 1.9
- first_shift: float32 [2048], P('shard'), may hold values from -1.75 to 1.75
- project_weight: bfloat16 [2048, 6144], P('shard'), may hold values from -0.125 to 0.125
- project_bias: float32 [6144], P('shard'), may hold values from -1.75 to 1.75
- mixing_weight: bfloat16 [2048, 2048], P('shard'), may hold values from -1 to 1
- mixing_bias: float32 [2048], P('shard'), may hold values from -1.75 to 1.75
- second_gain: float32 [2048], P('shard'), may hold values from 0.1 to 1.9
- second_shift: float32 [2048], P('shard'), may hold values from -1.75 to 1.75
- widen_weight: bfloat16 [2048, 8192], P('shard'), may hold values from -0.125 to 0.125
- widen_bias: float32 [8192], P('shard'), may hold values from -3 to 3
- narrow_weight: bfloat16 [8192, 2048], P('shard'), may hold values from -0.0625 to 0.0625
- narrow_bias: float32 [2048], P('shard'), may hold values from -1.75 to 1.75
- cotangent: bfloat16 [4096, 2048], P(('rep', 'shard')), may hold values from -6 to 6
Outputs:
- output: bfloat16 [4096, 2048], P(('rep', 'shard'))
- input_grad: bfloat16 [4096, 2048], P(('rep', 'shard'))
- first_gain_grad: float32 [2048], P('shard')
- first_shift_grad: float32 [2048], P('shard')
- project_weight_grad: float32 [2048, 6144], P('shard')
- project_bias_grad: float32 [6144], P('shard')
- mixing_weight_grad: float32 [2048, 2048], P('shard')
- mixing_bias_grad: float32 [2048], P('shard')
- second_gain_grad: float32 [2048], P('shard')
- second_shift_grad: float32 [2048], P('shard')
- widen_weight_grad: float32 [2048, 8192], P('shard')
- widen_bias_grad: float32 [8192], P('shard')
- narrow_weight_grad: float32 [8192, 2048], P('shard')
- narrow_bias_grad: float32 [2048], P('shard')
Inputs may be any that keep to these rules, and one draw needn't show every extreme that they name: `segment_ids`: documents never cross an aligned block of 128 tokens and begin only at positions within the block that are multiples of 8; in each block ids start at 0 and rise by one at each new document; some block holds 16 documents. `positions`: each token's position counts from 0 at the first token of its document; some block holds a single document.
All inputs are finite; a program needn't handle non-finite values.
Results may differ from a plain program's by a relative error of at most 0.015.
Values may be sent and summed in bfloat16 or wider, within the bound.
A program may use at most 640 MiB of HBM per device.

v0:
```python
import jax
import jax.numpy as jnp
from jax import lax
from jax.sharding import PartitionSpec as P

D = 2048
HEADS = 8
HEAD_DIM = 256
ROT = 64
FF = 8192


def layer_norm(values, gain, shift):
    center = values - jnp.mean(values, axis=-1, keepdims=True)
    spread = jnp.mean(center * center, axis=-1, keepdims=True)
    return center * lax.rsqrt(spread + 1e-05) * gain + shift


def angles(positions):
    freqs = 10000.0 ** (-(jnp.arange(ROT // 2, dtype=jnp.float32) * 2.0 / ROT))
    turned = positions.astype(jnp.float32)[..., None] * freqs
    return (jnp.cos(turned), jnp.sin(turned))


def rotary(values, cosine, sine):
    half = ROT // 2
    front = values[..., :half]
    back = values[..., half:ROT]
    return jnp.concatenate(
        [front * cosine - back * sine, back * cosine + front * sine, values[..., ROT:]], axis=-1
    )


def exact_gelu(values):
    return jax.nn.gelu(values, approximate=False)


def contract_rows(left, right):
    return lax.dot_general(
        left, right, (((0,), (0,)), ((), ())), preferred_element_type=jnp.float32
    )


def times_rows(left, piece):
    return lax.dot_general(
        left, piece, (((1,), (1,)), ((), ())), preferred_element_type=jnp.float32
    )


def weight_terms(left_one, left_two, left_mix, left_act, d_joint, d_widened, cotangent):

    def wide_term(start, count):
        return jnp.concatenate(
            [
                contract_rows(left_one, d_joint),
                contract_rows(left_two, d_widened),
                contract_rows(left_mix, cotangent),
            ],
            axis=1,
        )

    def down_term(start, count):
        return contract_rows(left_act, cotangent)

    return (wide_term, down_term)


def per_device(
    tokens,
    segment_ids,
    positions,
    first_gain,
    first_shift,
    project_weight,
    project_bias,
    mixing_weight,
    mixing_bias,
    second_gain,
    second_shift,
    widen_weight,
    widen_bias,
    narrow_weight,
    narrow_bias,
    cotangent,
):
    length = tokens.shape[0]
    shards = lax.axis_size("shard")
    gain_one, shift_one, gain_two, shift_two, joint_bias, mix_bias, wide_bias, narrow_full = (
        lax.all_gather(first_gain, "shard", axis=0, tiled=True),
        lax.all_gather(first_shift, "shard", axis=0, tiled=True),
        lax.all_gather(second_gain, "shard", axis=0, tiled=True),
        lax.all_gather(second_shift, "shard", axis=0, tiled=True),
        lax.all_gather(project_bias, "shard", axis=0, tiled=True),
        lax.all_gather(mixing_bias, "shard", axis=0, tiled=True),
        lax.all_gather(widen_bias, "shard", axis=0, tiled=True),
        lax.all_gather(narrow_bias, "shard", axis=0, tiled=True),
    )
    inputs = tokens.astype(jnp.float32)
    first_norm, first_pull = jax.vjp(layer_norm, inputs, gain_one, shift_one)
    second_norm, second_pull = jax.vjp(layer_norm, inputs, gain_two, shift_two)
    first = first_norm.astype(jnp.bfloat16)
    second = second_norm.astype(jnp.bfloat16)
    pieces = (
        lax.all_gather(project_weight, "shard", axis=0, tiled=True),
        lax.all_gather(widen_weight, "shard", axis=0, tiled=True),
    )
    part_one = jnp.dot(first, pieces[0], preferred_element_type=jnp.float32)
    part_two = jnp.dot(second, pieces[1], preferred_element_type=jnp.float32)
    joint = part_one + joint_bias
    widened = part_two + wide_bias
    shaped = joint.reshape(length, 3, HEADS, HEAD_DIM)
    cosine, sine = angles(positions)
    cosine = cosine[:, None, :]
    sine = sine[:, None, :]

    def place(query_in, key_in):
        return (rotary(query_in, cosine, sine) * HEAD_DIM ** (-0.5), rotary(key_in, cosine, sine))

    (query_turned, key_turned), rotate_pull = jax.vjp(place, shaped[:, 0], shaped[:, 1])
    query = query_turned.astype(jnp.bfloat16)
    keys = key_turned.astype(jnp.bfloat16)
    values = shaped[:, 2].astype(jnp.bfloat16)
    order = jnp.arange(length)
    allowed = ((segment_ids[:, None] == segment_ids[None, :]) & (order[:, None] >= order[None, :]))[
        None
    ]

    def masked_scores():
        raw = jnp.einsum("qhe,khe->hqk", query, keys, preferred_element_type=jnp.float32)
        return jnp.where(allowed, raw, -1e30)

    scores = masked_scores()
    highest = jnp.max(scores, axis=-1, keepdims=True)
    raised = jnp.exp(scores - highest)
    summed = jnp.sum(raised, axis=-1, keepdims=True)
    log_summed = highest + jnp.log(summed)
    weights = (raised / summed).astype(jnp.bfloat16)
    context = (
        jnp.einsum("hqk,khe->qhe", weights, values, preferred_element_type=jnp.float32)
        .reshape(length, D)
        .astype(jnp.bfloat16)
    )
    attention = (
        jnp.dot(
            context,
            lax.all_gather(mixing_weight, "shard", axis=0, tiled=True),
            preferred_element_type=jnp.float32,
        )
        + mix_bias
    )
    active_full, gelu_pull = jax.vjp(exact_gelu, widened)
    active = active_full.astype(jnp.bfloat16)
    mlp = (
        jnp.dot(
            active,
            lax.all_gather(narrow_weight, "shard", axis=0, tiled=True),
            preferred_element_type=jnp.float32,
        )
        + narrow_full
    )
    output = (inputs + attention + mlp).astype(jnp.bfloat16)

    def back_rows(piece):
        return times_rows(cotangent, piece)

    d_active = back_rows(lax.all_gather(narrow_weight, "shard", axis=0, tiled=True))
    d_widened = gelu_pull(d_active)[0].astype(jnp.bfloat16)
    d_context = back_rows(lax.all_gather(mixing_weight, "shard", axis=0, tiled=True))
    d_context = d_context.astype(jnp.bfloat16).reshape(length, HEADS, HEAD_DIM)
    again = jnp.exp(masked_scores() - log_summed)
    again_low = again.astype(jnp.bfloat16)
    d_weights = jnp.einsum("qhe,khe->hqk", d_context, values, preferred_element_type=jnp.float32)
    d_values = jnp.einsum("hqk,qhe->khe", again_low, d_context, preferred_element_type=jnp.float32)
    d_scores = (again * (d_weights - jnp.sum(d_weights * again, axis=-1, keepdims=True))).astype(
        jnp.bfloat16
    )
    d_query = jnp.einsum("hqk,khe->qhe", d_scores, keys, preferred_element_type=jnp.float32)
    d_keys = jnp.einsum("hqk,qhe->khe", d_scores, query, preferred_element_type=jnp.float32)
    d_query_in, d_key_in = rotate_pull((d_query, d_keys))
    d_joint = jnp.concatenate(
        [d_query_in.reshape(length, D), d_key_in.reshape(length, D), d_values.reshape(length, D)],
        axis=1,
    ).astype(jnp.bfloat16)
    pieces = lax.all_gather((project_weight, widen_weight), "shard", axis=0, tiled=True)
    stacked = jnp.concatenate(
        [times_rows(d_joint, pieces[0]), times_rows(d_widened, pieces[1])], axis=0
    )
    d_in_one, d_gain_one, d_shift_one = first_pull(stacked[:length])
    d_in_two, d_gain_two, d_shift_two = second_pull(stacked[length:])
    input_grad = (cotangent.astype(jnp.float32) + d_in_one + d_in_two).astype(jnp.bfloat16)
    sums = lax.psum(
        (
            d_gain_one,
            d_shift_one,
            d_gain_two,
            d_shift_two,
            jnp.sum(d_joint, axis=0, dtype=jnp.float32),
            jnp.sum(cotangent, axis=0, dtype=jnp.float32),
            jnp.sum(d_widened, axis=0, dtype=jnp.float32),
        ),
        ("rep", "shard"),
    )
    owner = lax.axis_index("shard")

    def own_part(vector):
        share = vector.shape[0] // shards
        return lax.dynamic_slice_in_dim(vector, owner * share, share)

    owned = [own_part(vector) for vector in sums]
    wide_term, down_term = weight_terms(
        first, second, context, active, d_joint, d_widened, cotangent
    )
    wide_part = lax.psum_scatter(
        wide_term(jnp.int32(0), lax.axis_size("shard") * (D // shards)).astype(jnp.bfloat16),
        "shard",
        scatter_dimension=0,
        tiled=True,
    ).astype(jnp.float32)
    down_part = lax.psum_scatter(
        down_term(jnp.int32(0), lax.axis_size("shard") * (FF // shards)).astype(jnp.bfloat16),
        "shard",
        scatter_dimension=0,
        tiled=True,
    ).astype(jnp.float32)
    wide_part, down_part = (
        lax.psum(wide_part.astype(jnp.bfloat16), "rep").astype(jnp.float32),
        lax.psum(down_part.astype(jnp.bfloat16), "rep").astype(jnp.float32),
    )
    return (
        output,
        input_grad,
        owned[0],
        owned[1],
        wide_part[:, : 3 * D],
        owned[4],
        wide_part[:, 3 * D + FF :],
        owned[5],
        owned[2],
        owned[3],
        wide_part[:, 3 * D : 3 * D + FF],
        owned[6],
        down_part,
        owned[5],
    )


def solution(mesh):
    in_specs = (
        P(("rep", "shard"), None),
        P(("rep", "shard")),
        P(("rep", "shard")),
        P("shard"),
        P("shard"),
        P("shard", None),
        P("shard"),
        P("shard", None),
        P("shard"),
        P("shard"),
        P("shard"),
        P("shard", None),
        P("shard"),
        P("shard", None),
        P("shard"),
        P(("rep", "shard"), None),
    )
    out_specs = (
        P(("rep", "shard"), None),
        P(("rep", "shard"), None),
        P("shard"),
        P("shard"),
        P("shard", None),
        P("shard"),
        P("shard", None),
        P("shard"),
        P("shard"),
        P("shard"),
        P("shard", None),
        P("shard"),
        P("shard", None),
        P("shard"),
    )
    return jax.shard_map(
        per_device, mesh=mesh, in_specs=in_specs, out_specs=out_specs, check_vma=False
    )
```

profile of v0, /device:TPU:29, one launch (start us, length us, event | category | flops | bytes accessed | tf_op | source)
XLA Modules:
  0.0 3882.6 jit_solution(1283411526838267227)
XLA Ops:
  7.2 0.7 all-gather.16.cloned.1.call-update
  8.0 0.7 all-gather.18.cloned.1.call-update
  8.7 0.7 all-gather.14.cloned.1.call-update
  10.1 55.4 %all-gather.4 = f32[8,1,256]{2,1,0:T(1,128)S(1)} all-gather(f32[1,1,256]{2,1,0:T(1,128)S(1)} %bitcast.99), channel_id=1, replica_groups=mesh['rep'=4,'shard'=8] {'shard'}, dimensions={0}, use_global_device_ids=true | all-gather | bytes 9216 | tf_op jit(solution)/shard_map/all_gather | solution.py:91
  65.5 22.6 all-gather.5
  88.2 32.9 all_gather.49
  121.5 526.6 %all-gather.16.cloned.1.call-done = bf16[2048,8192]{1,0:T(8,128)(2,1)} async-done(((bf16[256,8192]{1,0:T(8,128)(2,1)}), bf16[2048,8192]{1,0:T(8,128)(2,1)}) %all-gather.16.cloned.1.call-update) | async-done | bytes 33554448 | tf_op jit(solution)/shard_map/all_gather | solution.py:105
  648.1 17.7 convolution_add_fusion
  665.8 621.6 %all-gather.18.cloned.1.call-done = bf16[8192,2048]{1,0:T(8,128)(2,1)} async-done(((bf16[1024,2048]{1,0:T(8,128)(2,1)}), bf16[8192,2048]{1,0:T(8,128)(2,1)}) %all-gather.18.cloned.1.call-update) | async-done | bytes 33554448 | tf_op jit(solution)/shard_map/all_gather | solution.py:156
  1287.4 27.1 convert_reduce_fusion
  1314.5 3.9 multiply_convert_fusion
  1318.5 1.3 copy-done.1
  1319.8 13.8 convolution_convert_fusion.1
  1334.3 12.7 all-gather
  1346.9 15.6 all-gather.1
  1362.6 24.5 all-gather.2
  1387.5 25.8 all-gather.14.cloned.1.call-done
  1413.3 7.1 convolution_convert_fusion.4
  1420.3 2.0 copy.91
  1422.4 472.7 %all-gather.12.cloned.1.call-done = bf16[2048,6144]{1,0:T(8,128)(2,1)} async-done(((bf16[256,6144]{1,0:T(8,128)(2,1)}), bf16[2048,6144]{1,0:T(8,128)(2,1)}) %all-gather.12.cloned.1.call-update) | async-done | bytes 25165840 | tf_op jit(solution)/shard_map/all_gather | solution.py:104
  1895.1 10.3 convolution_add_fusion.1
  1905.4 1.0 copy.93
  1906.4 1.8 copy-done.3
  1908.2 1.2 copy.92
  1909.4 1.7 fusion.55
  1912.8 0.7 fusion.31
  1915.3 0.7 fusion.19
  1915.9 1.3 split.24
  1917.2 1.3 multiply_add_fusion.3
  1918.5 1.4 add_convert_fusion.1
  1920.0 2.1 copy.75
  1922.0 3.0 add_convert_fusion.2
  1925.0 2.0 copy.71
  1927.1 2.2 convolution_convert_fusion.5
  1929.3 1.3 convolution_convert_fusion.6
  1930.7 5.7 convolution_convert_fusion.3
  1936.4 13.5 convolution_convert_fusion.2
  1949.9 13.9 convolution_convert_fusion
  1963.9 44.6 %pad_maximum_fusion = bf16[2048,16384]{1,0:T(8,128)(2,1)} fusion(bf16[2048,2048]{1,0:T(8,128)(2,1)} %convolution_convert_fusion.3, bf16[2048,8192]{1,0:T(8,128)(2,1)} %convolution_convert_fusion, bf16[2048,6144]{1,0:T(8,128)(2,1)} %convolution_convert_fusion.2), kind=kLoop, calls=%fused_computation | loop fusion | flops 201326592 | bytes 134217728 | tf_op jit(solution)/shard_map/concatenate | solution.py:53
  2008.5 2.3 convert_reduce_fusion.1
  2010.8 17.4 fusion.57
  2028.2 15.3 fusion.53
  2043.6 2.8 fusion.27
  2046.4 3.6 convert_reduce_fusion.3
  2050.0 391.7 %reduce-scatter.5.cloned.1.call-done = bf16[1024,2048]{1,0:T(8,128)(2,1)} async-done(((bf16[8192,2048]{1,0:T(8,128)(2,1)}), bf16[1024,2048]{1,0:T(8,128)(2,1)}) %reduce-scatter.5.cloned.1.call-update) | async-done | bytes 4194320 | tf_op jit(solution)/shard_map/reduce_scatter | solution.py:219
  2441.7 1058.8 %reduce-scatter.3.cloned.1.call-done = bf16[256,16384]{1,0:T(8,128)(2,1)} async-done(((bf16[2048,16384]{1,0:T(8,128)(2,1)}), bf16[256,16384]{1,0:T(8,128)(2,1)}) %reduce-scatter.3.cloned.1.call-update) | async-done | bytes 8388624 | tf_op jit(solution)/shard_map/reduce_scatter | solution.py:213
  3500.5 0.6 copy-done.24
  3501.2 12.5 all-gather.3
  3513.7 14.9 all-gather.6
  3528.6 4.9 fusion.7
  3533.5 14.2 fusion.8
  3547.7 84.5 %all-reduce.11.cloned.1.call-done = (f32[2048]{0:T(1024)}, f32[2048]{0:T(1024)}, f32[6144]{0:T(1024)}, f32[2048]{0:T(1024)}, f32[2048]{0:T(1024)}, /*index=5*/f32[2048]{0:T(1024)}, f32[8192]{0:T(1024)}) async-done(((f32[2048]{0:T(1024)}, f32[2048]{0:T(1024)}, f32[6144]{0:T(1024)}, f32[2048]{0:T(1024)}, f32[2048]{0:T(1024)}, /*index=5*/f32[2048]{0:T(1024)}, f32[8192]{0:T(1024)}), (f32[2048]{0:T(1024)}, ...) | async-done | bytes 98320 | tf_op jit(solution)/shard_map/psum | solution.py:191
  3632.2 1.3 dynamic_slice.21
  3633.5 0.8 dynamic_slice.24
  3634.3 1.3 dynamic_slice.22
  3635.6 1.3 dynamic_slice.25
  3636.9 1.3 dynamic_slice.26
  3638.2 1.3 dynamic_slice.23
  3639.5 1.3 dynamic_slice.27
  3640.8 216.6 %all-reduce.13.cloned.1.call-done = (bf16[256,16384]{1,0:T(8,128)(2,1)}, bf16[1024,2048]{1,0:T(8,128)(2,1)}) async-done(((bf16[256,16384]{1,0:T(8,128)(2,1)}, bf16[1024,2048]{1,0:T(8,128)(2,1)}), (bf16[256,16384]{1,0:T(8,128)(2,1)}, bf16[1024,2048]{1,0:T(8,128)(2,1)})) %all-reduce.13.cloned.1.call-update) | async-done | bytes 12582928 | tf_op jit(solution)/shard_map/psum | solution.py:226
  3857.4 2.9 slice.60
  3860.3 5.5 slice.59
  3865.8 4.4 slice.61
  3870.2 4.4 convert_element_type.100
  (95 shorter events, 6.5 us)
Async XLA Ops:
  7.2 640.9 %all-gather.16.cloned.1.call-start = ((), (), s32[]{:S(2)}) async-start(), calls=%async_computation.4 | async-start | bytes 37748736 | tf_op jit(solution)/shard_map/all_gather | solution.py:105
  7.9 2.1 copy-start.20
  7.9 57.6 %copy-start.21 = (f32[256]{0:T(256)S(1)}, f32[256]{0:T(256)}, u32[]{:S(2)}) copy-start(f32[256]{0:T(256)} %param.26) | copy-start | bytes 3076
  7.9 80.2 %copy-start.14 = (f32[1024]{0:T(1024)S(1)}, f32[1024]{0:T(1024)}, u32[]{:S(2)}) copy-start(f32[1024]{0:T(1024)} %param.28) | copy-start | bytes 12292
  7.9 113.1 %copy-start = (bf16[128,2048]{1,0:T(8,128)(2,1)S(1)}, bf16[128,2048]{1,0:T(8,128)(2,1)}, u32[]{:S(2)}) copy-start(bf16[128,2048]{1,0:T(8,128)(2,1)} %param.16) | copy-start | bytes 1572868
  8.0 1279.4 %all-gather.18.cloned.1.call-start = ((), (), s32[]{:S(2)}) async-start(), calls=%async_computation.5 | async-start | bytes 37748736 | tf_op jit(solution)/shard_map/all_gather | solution.py:156
  8.7 1404.6 %all-gather.14.cloned.1.call-start = ((), (), s32[]{:S(2)}) async-start(), calls=%async_computation.3 | async-start | bytes 9437184 | tf_op jit(solution)/shard_map/all_gather | solution.py:146
  9.4 1885.7 %all-gather.12.cloned.1.call-start = ((), (), s32[]{:S(2)}) async-start(), calls=%async_computation.2 | async-start | bytes 28311552 | tf_op jit(solution)/shard_map/all_gather | solution.py:104
  10.0 2431.7 %reduce-scatter.5.cloned.1.call-start = ((), (), s32[]{:S(2)}) async-start(), calls=%async_computation.7 | async-start | bytes 37748736 | tf_op jit(solution)/shard_map/reduce_scatter | solution.py:219
  121.5 544.3 %copy-start.18 = (f32[128]{0:T(128)}, f32[128]{0:T(128)S(1)}, u32[]{:S(2)}) copy-start(f32[128]{0:T(128)S(1)} %fusion.28) | copy-start | bytes 1540
  648.1 639.3 %copy-start.5 = (bf16[128,2048]{1,0:T(8,128)(2,1)S(1)}, bf16[128,2048]{1,0:T(8,128)(2,1)}, u32[]{:S(2)}) copy-start(bf16[128,2048]{1,0:T(8,128)(2,1)} %param.31) | copy-start | bytes 1572868
  1318.5 1.3 copy-start.1
  1333.6 0.7 copy-start.26
  1333.6 0.7 copy-start.15
  1333.6 0.7 copy-start.22
  1333.6 13.4 copy-start.23
  1333.6 53.5 %copy-start.17 = (s32[128]{0:T(128)S(1)}, s32[128]{0:T(128)}, u32[]{:S(2)}) copy-start(s32[128]{0:T(128)} %param.17) | copy-start | bytes 1540
  1333.6 2166.9 %reduce-scatter.3.cloned.1.call-start = ((), (), s32[]{:S(2)}) async-start(), calls=%async_computation.6 | async-start | bytes 75497472 | tf_op jit(solution)/shard_map/reduce_scatter | solution.py:213
  1906.4 1.8 copy-start.3
  1912.3 1.8 copy-start.11
  1912.3 1.8 copy-start.13
  1927.1 3.6 copy-start.6
  1930.7 5.8 copy-start.8
  1930.7 5.7 copy-start.10
  2008.5 1623.7 %all-reduce.11.cloned.1.call-start = ((), (), s32[]{:S(2)}) async-start(), calls=%async_computation.8 | async-start | bytes 196608 | tf_op jit(solution)/shard_map/psum | solution.py:191
  2028.2 15.3 copy-start.19
  2028.2 15.3 copy-start.4
  2028.2 18.1 copy-start.7
  2050.0 1807.4 %all-reduce.13.cloned.1.call-start = ((), (), s32[]{:S(2)}) async-start(), calls=%async_computation.9 | async-start | bytes 25165824 | tf_op jit(solution)/shard_map/psum | solution.py:226
  3500.5 0.7 copy-start.24
  3500.5 13.2 copy-start.25
  3500.5 28.1 copy-start.9
  3528.6 4.9 copy-start.2
  3634.3 240.4 %copy-start.16 = (f32[256]{0:T(256)}, f32[256]{0:T(256)S(1)}, u32[]{:S(2)}) copy-start(f32[256]{0:T(256)S(1)} %dynamic_slice.24) | copy-start | bytes 3076
  3857.4 8.4 slice-start
  3860.3 5.5 slice-start.1
  3865.8 4.4 copy-start.12
Sparse Core Ops, SparseCore 0:
  9.5 638.5 all-gather.15
  649.6 637.6 all-gather.17
  1289.5 123.7 all-gather.13
  1414.7 480.4 all-gather.11
  1898.7 542.9 reduce-scatter.4
  2445.3 1055.1 reduce-scatter.2
  3508.1 124.0 all-reduce.10
  3635.0 222.3 all-reduce.12
where the time goes:
time: 3890 us; the launch traced here: 3880 us
  waiting for transfers between devices  3400 us (87%)
  blocking collectives  191 us (5%)
  matrix products  166 us (4%)
  other arithmetic  69.6 us (2%)
  local copies, waits for them, and re-layouts  39.3 us (1%)
    reduce_scatter x1, waiting for transfers between devices, per_device(): lax.psum_scatter(wide_term(jnp.int32(0), lax.axis_size('shard') * (D // s...  1060 us
    all_gather x1, waiting for transfers between devices, per_device(): lax.all_gather(narrow_weight, 'shard', axis=0, tiled=True)  622 us
    all_gather x1, waiting for transfers between devices, per_device(): lax.all_gather(widen_weight, 'shard', axis=0, tiled=True)  527 us
    all_gather x1, waiting for transfers between devices, per_device(): lax.all_gather(project_weight, 'shard', axis=0, tiled=True)  473 us
    reduce_scatter x1, waiting for transfers between devices, per_device(): lax.psum_scatter(down_term(jnp.int32(0), lax.axis_size('shard') * (FF //...  392 us
    psum x1, waiting for transfers between devices, per_device(): lax.psum(wide_part.astype(jnp.bfloat16), 'rep').astype(jnp.float32)  217 us
    psum x1, waiting for transfers between devices, per_device(): lax.psum((d_gain_one, d_shift_one, d_gain_two, d_shift_two, jnp.sum(d_joi...  84.5 us
  transfers between devices with their start and end apart: 8, of which 8 were waited for; matrix products, arithmetic and copies ran while one was open for 7% of the time, Pallas kernels for 0%

commit v1 on v0

--- a/solution.py
+++ b/solution.py
@@ -1,6 +1,8 @@
 import jax
 import jax.numpy as jnp
 from jax import lax
+from jax.experimental import pallas as pl
+from jax.experimental.pallas import tpu as pltpu
 from jax.sharding import PartitionSpec as P
 
 D = 2048
@@ -244,7 +246,865 @@
     )
 
 
+MESH = pl.DeviceIdType.MESH
+ANY = pl.BlockSpec(memory_space=pl.ANY)
+
+
+def places():
+    rep, me = lax.axis_index("rep"), lax.axis_index("shard")
+    core, side = rep % 2, rep // 2
+    col, line = me % 2, me // 2
+    return rep, me, core, side, col, line
+
+
+def greet(peers):
+    barrier = pltpu.get_barrier_semaphore()
+    for peer in peers:
+        pl.semaphore_signal(barrier, inc=1, device_id=peer, device_id_type=MESH)
+    pl.semaphore_wait(barrier, len(peers))
+
+
+def remote(source, target, send, recv, device):
+    return pltpu.make_async_remote_copy(
+        src_ref=source,
+        dst_ref=target,
+        send_sem=send,
+        recv_sem=recv,
+        device_id=device,
+        device_id_type=MESH,
+    )
+
+
+def spread_kernel(
+    tok, cot, wide_one, wide_two, small,
+    tok_all, cot_all, cols_one, cols_two, small_all,
+    line_send, line_recv, col_send, col_recv,
+    own_sem, piece_send, piece_recv, side_send, side_recv, core_send, core_recv,
+    small_send, small_recv,
+):
+    rep, me, core, side, col, line = places()
+    twin = rep + 1 - 2 * core
+    across = rep + 2 - 4 * side
+    other = me + 1 - 2 * col
+    wide = cols_one.shape[1] // 3
+    two_wide = cols_two.shape[1]
+    rows = wide_one.shape[0]
+    share = rows // 4
+    greet(
+        [(rep, (me + step) % 8) for step in range(1, 8)]
+        + [(twin, me), (across, me)]
+    )
+
+    def block(array, index):
+        return array.at[index]
+
+    def along(which, array, gathered, direction, step):
+        owner = line - direction * (step - 1)
+        source = array if step == 1 else gathered.at[owner * 2 + col]
+        lane = which * 6 + (0 if direction == 1 else 3) + step - 1
+        return remote(
+            source,
+            gathered.at[owner * 2 + col],
+            line_send.at[lane],
+            line_recv.at[lane],
+            (rep, (line + direction) * 2 + col),
+        )
+
+    def sends(direction, step):
+        if direction == 1:
+            return (line >= step - 1) & (line <= 2)
+        return (line <= 4 - step) & (line >= 1)
+
+    def gets(direction, step):
+        if direction == 1:
+            return line >= step
+        return line <= 3 - step
+
+    def sideways(which, array, gathered, direction, step):
+        owner = line - direction * step
+        source = array if step == 0 else gathered.at[owner * 2 + col]
+        lane = which * 7 + (0 if direction == 1 else 3) + step
+        return remote(
+            source,
+            gathered.at[owner * 2 + col],
+            col_send.at[lane],
+            col_recv.at[lane],
+            (rep, other),
+        )
+
+    def from_other(which, gathered, direction, step):
+        owner = line - direction * step
+        lane = which * 7 + (0 if direction == 1 else 3) + step
+        return remote(
+            gathered.at[owner * 2 + 1 - col],
+            gathered.at[owner * 2 + 1 - col],
+            col_send.at[lane],
+            col_recv.at[lane],
+            (rep, other),
+        )
+
+    pairs = ((tok, tok_all), (cot, cot_all))
+    turns = [(direction, step) for step in (1, 2, 3) for direction in (1, -1)]
+
+    def begin(which):
+        array, gathered = pairs[which]
+        for direction in (1, -1):
+            @pl.when(sends(direction, 1))
+            def _(direction=direction):
+                along(which, array, gathered, direction, 1).start()
+        sideways(which, array, gathered, 1, 0).start()
+
+    def pass_on(which):
+        array, gathered = pairs[which]
+        for direction, step in turns:
+            @pl.when(gets(direction, step))
+            def _(direction=direction, step=step):
+                owner = line - direction * step
+                lane = which * 6 + (0 if direction == 1 else 3) + step - 1
+                here = gathered.at[owner * 2 + col]
+                remote(
+                    here, here, line_send.at[lane], line_recv.at[lane], (rep, me)
+                ).wait_recv()
+                sideways(which, array, gathered, direction, step).start()
+
+            if step < 3:
+                @pl.when(sends(direction, step + 1))
+                def _(direction=direction, step=step):
+                    along(which, array, gathered, direction, step + 1).start()
+
+    def finish(which):
+        array, gathered = pairs[which]
+        for direction, step in turns:
+            @pl.when(sends(direction, step))
+            def _(direction=direction, step=step):
+                along(which, array, gathered, direction, step).wait_send()
+
+            @pl.when(gets(direction, step))
+            def _(direction=direction, step=step):
+                sideways(which, array, gathered, direction, step).wait_send()
+                from_other(which, gathered, direction, step).wait_recv()
+
+        sideways(which, array, gathered, 1, 0).wait_send()
+        from_other(which, gathered, 1, 0).wait_recv()
+
+    mine = pl.multiple_of(rep * share, share)
+
+    def pieces(step):
+        target = (me + step) % 8
+        place = pl.ds(pl.multiple_of(me * rows + rep * share, share), share)
+        out = []
+        for part in range(3):
+            out.append(
+                remote(
+                    wide_one.at[
+                        pl.ds(mine, share),
+                        pl.ds(pl.multiple_of((part * 8 + target) * wide, wide), wide),
+                    ],
+                    cols_one.at[place, pl.ds(part * wide, wide)],
+                    piece_send.at[step - 1, part],
+                    piece_recv.at[step - 1, part],
+                    (rep, target),
+                )
+            )
+        out.append(
+            remote(
+                wide_two.at[
+                    pl.ds(mine, share),
+                    pl.ds(pl.multiple_of(target * two_wide, two_wide), two_wide),
+                ],
+                cols_two.at[place, :],
+                piece_send.at[step - 1, 3],
+                piece_recv.at[step - 1, 3],
+                (rep, target),
+            )
+        )
+        return out
+
+    def arrived(step):
+        source = (me + 8 - step) % 8
+        place = pl.ds(pl.multiple_of(source * rows + rep * share, share), share)
+        out = []
+        for part in range(3):
+            here = cols_one.at[place, pl.ds(part * wide, wide)]
+            out.append(
+                remote(
+                    here, here, piece_send.at[step - 1, part],
+                    piece_recv.at[step - 1, part], (rep, source),
+                )
+            )
+        here = cols_two.at[place, :]
+        out.append(
+            remote(
+                here, here, piece_send.at[step - 1, 3], piece_recv.at[step - 1, 3],
+                (rep, source),
+            )
+        )
+        return out
+
+    def shares(step, quarter, send, recv, lane, device):
+        source = (me + 8 - step) % 8
+        place = pl.ds(pl.multiple_of(source * rows + quarter * share, share), share)
+        return [
+            remote(
+                array.at[place, :], array.at[place, :],
+                send.at[lane, step - 1, index], recv.at[lane, step - 1, index], device,
+            )
+            for index, array in enumerate((cols_one, cols_two))
+        ]
+
+    def little(step):
+        return remote(
+            small, small_all.at[me], small_send.at[step - 1], small_recv.at[step - 1],
+            (rep, (me + step) % 8),
+        )
+
+    begin(0)
+    for step in range(1, 8):
+        little(step).start()
+    for step in range(1, 8):
+        for copy in pieces(step):
+            copy.start()
+    own = [
+        pltpu.make_async_copy(tok, tok_all.at[me], own_sem.at[0]),
+        pltpu.make_async_copy(cot, cot_all.at[me], own_sem.at[1]),
+        pltpu.make_async_copy(small, small_all.at[me], own_sem.at[2]),
+        pltpu.make_async_copy(
+            wide_two.at[:, pl.ds(pl.multiple_of(me * two_wide, two_wide), two_wide)],
+            cols_two.at[pl.ds(pl.multiple_of(me * rows, rows), rows), :],
+            own_sem.at[3],
+        ),
+    ] + [
+        pltpu.make_async_copy(
+            wide_one.at[:, pl.ds(pl.multiple_of((part * 8 + me) * wide, wide), wide)],
+            cols_one.at[
+                pl.ds(pl.multiple_of(me * rows, rows), rows), pl.ds(part * wide, wide)
+            ],
+            own_sem.at[4 + part],
+        )
+        for part in range(3)
+    ]
+    for copy in own:
+        copy.start()
+    pass_on(0)
+    begin(1)
+    for step in range(1, 8):
+        for copy in arrived(step):
+            copy.wait_recv()
+        for copy in shares(step, rep, side_send, side_recv, 0, (across, me)):
+            copy.start()
+        for copy in shares(step, rep, core_send, core_recv, 0, (twin, me)):
+            copy.start()
+    pass_on(1)
+    for step in range(1, 8):
+        for copy in shares(step, across, side_send, side_recv, 0, (across, me)):
+            copy.wait_recv()
+        for copy in shares(step, across, core_send, core_recv, 1, (twin, me)):
+            copy.start()
+    finish(0)
+    finish(1)
+    twin_across = across + 1 - 2 * core
+    for step in range(1, 8):
+        for copy in pieces(step):
+            copy.wait_send()
+        for copy in shares(step, rep, side_send, side_recv, 0, (across, me)):
+            copy.wait_send()
+        for copy in shares(step, rep, core_send, core_recv, 0, (twin, me)):
+            copy.wait_send()
+        for copy in shares(step, across, core_send, core_recv, 1, (twin, me)):
+            copy.wait_send()
+        for copy in shares(step, twin, core_send, core_recv, 0, (twin, me)):
+            copy.wait_recv()
+        for copy in shares(step, twin_across, core_send, core_recv, 1, (twin, me)):
+            copy.wait_recv()
+        source = (me + 8 - step) % 8
+        little(step).wait_send()
+        remote(
+            small_all.at[source], small_all.at[source], small_send.at[step - 1],
+            small_recv.at[step - 1], (rep, source),
+        ).wait_recv()
+    for copy in own:
+        copy.wait()
+
+
+def spread(tok, cot, wide_one, wide_two, small):
+    dma = pltpu.SemaphoreType.DMA
+    length, width = tok.shape
+    rows, one = wide_one.shape
+    two = wide_two.shape[1]
+    bf16 = jnp.bfloat16
+    return pl.pallas_call(
+        spread_kernel,
+        out_shape=(
+            jax.ShapeDtypeStruct((8, length, width), bf16),
+            jax.ShapeDtypeStruct((8, length, width), bf16),
+            jax.ShapeDtypeStruct((rows * 8, one // 8), bf16),
+            jax.ShapeDtypeStruct((rows * 8, two // 8), bf16),
+            jax.ShapeDtypeStruct((8,) + small.shape, jnp.float32),
+        ),
+        in_specs=[ANY] * 5,
+        out_specs=(ANY,) * 5,
+        scratch_shapes=[
+            dma((12,)), dma((12,)), dma((14,)), dma((14,)),
+            dma((7,)), dma((7, 4)), dma((7, 4)),
+            dma((1, 7, 2)), dma((1, 7, 2)), dma((2, 7, 2)), dma((2, 7, 2)),
+            dma((7,)), dma((7,)),
+        ],
+        compiler_params=pltpu.CompilerParams(collective_id=0, has_side_effects=True),
+        name="spread",
+    )(tok, cot, wide_one, wide_two, small)
+
+
+def rows_loop(extent, chunk, body):
+    @pl.loop(0, extent // chunk)
+    def _(index):
+        body(pl.ds(pl.multiple_of(index * chunk, chunk), chunk))
+
+
+def add_two(target, left, right, chunk):
+    def body(rows):
+        target[rows, :] = (
+            left[rows, :].astype(jnp.float32) + right[rows, :].astype(jnp.float32)
+        ).astype(target.dtype)
+
+    rows_loop(target.shape[0], chunk, body)
+
+
+def add_three(target, left, right, third, chunk):
+    def body(rows):
+        target[rows, :] = (
+            left[rows, :].astype(jnp.float32)
+            + right[rows, :].astype(jnp.float32)
+            + third[rows, :].astype(jnp.float32)
+        ).astype(target.dtype)
+
+    rows_loop(target.shape[0], chunk, body)
+
+
+def gather_sums_kernel(
+    out_part, in_part, one, two, mix, narrow, vec,
+    out_sum, in_sum, one_full, two_full, mix_full, narrow_full, vec_full,
+    loc_one, loc_two, loc_mix, loc_nar,
+    core_one, core_two, core_mix, core_nar,
+    side_one, side_two, side_mix, side_nar,
+    loc_act, col_act, line_act, total, vec_loc, vec_got, vec_mid, vec_rep,
+    load_sem, cs, cr, ss, sr, ys, yr, zs, zr, ps, pr, fs, fr, vs, vr, us, ur, ds_sem,
+):
+    rep, me, core, side, col, line = places()
+    twin = rep + 1 - 2 * core
+    across = rep + 2 - 4 * side
+    diagonal = across + 1 - 2 * core
+    other = me + 1 - 2 * col
+    greet(
+        [(rep, (me + step) % 8) for step in range(1, 8)]
+        + [(twin, me), (across, me), (diagonal, me)]
+    )
+    grads = (
+        (one, loc_one, core_one, side_one),
+        (two, loc_two, core_two, side_two),
+        (mix, loc_mix, core_mix, side_mix),
+        (narrow, loc_nar, core_nar, side_nar),
+    )
+    acts = (out_part, in_part)
+
+    def quarter_of(index, quarter):
+        full = grads[index][0]
+        return full.at[:, quarter] if index < 2 else full.at[quarter]
+
+    def core_copy(index, slot):
+        full, _, got, _ = grads[index]
+        quarter = (across if slot == 0 else rep) + 1 - 2 * core
+        return remote(
+            quarter_of(index, quarter), got.at[slot], cs.at[index, slot], cr.at[index, slot],
+            (twin, me),
+        )
+
+    def load(index, slot):
+        full, local, _, _ = grads[index]
+        quarter = across if slot == 0 else rep
+        return pltpu.make_async_copy(
+            quarter_of(index, quarter), local.at[slot], load_sem.at[index, slot]
+        )
+
+    def side_copy(index):
+        _, local, _, got = grads[index]
+        return remote(local.at[0], got, ss.at[index], sr.at[index], (across, me))
+
+    def col_copy(index, step):
+        target = (line + step) % 4
+        return remote(
+            acts[index].at[target * 2 + 1 - col], col_act.at[index, step],
+            ys.at[index, step], yr.at[index, step], (rep, other),
+        )
+
+    def act_load(index, step):
+        target = (line + step) % 4
+        return pltpu.make_async_copy(
+            acts[index].at[target * 2 + col], loc_act.at[index, step],
+            load_sem.at[4 + index, step],
+        )
+
+    def line_copy(index, step):
+        return remote(
+            loc_act.at[index, step], line_act.at[index, step - 1],
+            zs.at[index, step - 1], zr.at[index, step - 1],
+            (rep, ((line + step) % 4) * 2 + col),
+        )
+
+    def vec_copy(step):
+        target = (me + step) % 8
+        return remote(
+            vec.at[target], vec_got.at[step - 1], vs.at[step - 1], vr.at[step - 1],
+            (rep, target),
+        )
+
+    def vec_share(step):
+        target = (rep + step) % 4
+        return remote(
+            vec_mid, vec_rep.at[step - 1], us.at[step - 1], ur.at[step - 1],
+            (target, me),
+        )
+
+    for index in (0, 1):
+        for slot in (0, 1):
+            core_copy(index, slot).start()
+            load(index, slot).start()
+    for index in (2, 3):
+        for slot in (0, 1):
+            core_copy(index, slot).start()
+            load(index, slot).start()
+    for step in range(1, 8):
+        vec_copy(step).start()
+    vec_load = pltpu.make_async_copy(vec.at[me], vec_loc, ds_sem.at[0])
+    vec_load.start()
+    for index in (0, 1):
+        for step in (2, 1, 3, 0):
+            col_copy(index, step).start()
+            act_load(index, step).start()
+
+    def flat(ref):
+        if len(ref.shape) == 3:
+            return [ref.at[i] for i in range(ref.shape[0])]
+        return [ref]
+
+    for index in range(4):
+        _, local, got, _ = grads[index]
+        core_copy(index, 0).wait_recv()
+        load(index, 0).wait()
+        for here, there in zip(flat(local.at[0]), flat(got.at[0])):
+            add_two(here, here, there, 16)
+        side_copy(index).start()
+
+    for index in (0, 1):
+        for step in (2, 1, 3):
+            col_copy(index, step).wait_recv()
+            act_load(index, step).wait()
+            here = loc_act.at[index, step]
+            add_two(here, here, col_act.at[index, step], 16)
+            line_copy(index, step).start()
+
+    vec_load.wait()
+    for step in range(1, 8):
+        vec_copy(step).wait_recv()
+    running = vec_loc[...]
+    for step in range(1, 8):
+        running = running + vec_got[step - 1]
+    vec_mid[...] = running
+    for step in range(1, 4):
+        vec_share(step).start()
+
+    share_one = one_full.shape[0] // 4
+    wide = loc_one.shape[3] // 3
+    two_wide = loc_two.shape[3]
+    my_rows = pl.ds(pl.multiple_of(rep * share_one, share_one), share_one)
+
+    def whole(index):
+        _, local, got, arrived = grads[index]
+        core_copy(index, 1).wait_recv()
+        load(index, 1).wait()
+        side_copy(index).wait_recv()
+        for here, there, far in zip(flat(local.at[1]), flat(got.at[1]), flat(arrived)):
+            add_three(here, here, there, far, 16)
+
+    def piece(index, step, part, source_shard, target_shard, local):
+        if index == 0:
+            return remote(
+                local.at[:, pl.ds(part * wide, wide)],
+                one_full.at[
+                    my_rows,
+                    pl.ds(pl.multiple_of((part * 8 + source_shard) * wide, wide), wide),
+                ],
+                ps.at[step, part], pr.at[step, part], (rep, target_shard),
+            )
+        return remote(
+            local,
+            two_full.at[
+                my_rows, pl.ds(pl.multiple_of(source_shard * two_wide, two_wide), two_wide)
+            ],
+            ps.at[step, 3], pr.at[step, 3], (rep, target_shard),
+        )
+
+    def pieces(index, step, source_shard, target_shard):
+        local = grads[index][1].at[1, target_shard]
+        parts = range(3) if index == 0 else (0,)
+        return [
+            piece(index, step, part, source_shard, target_shard, local) for part in parts
+        ]
+
+    def own_pieces(index):
+        if index == 0:
+            return [
+                pltpu.make_async_copy(
+                    loc_one.at[1, me, :, pl.ds(part * wide, wide)],
+                    one_full.at[
+                        my_rows,
+                        pl.ds(pl.multiple_of((part * 8 + me) * wide, wide), wide),
+                    ],
+                    ds_sem.at[1 + part],
+                )
+                for part in range(3)
+            ]
+        return [
+            pltpu.make_async_copy(
+                loc_two.at[1, me],
+                two_full.at[
+                    my_rows, pl.ds(pl.multiple_of(me * two_wide, two_wide), two_wide)
+                ],
+                ds_sem.at[4],
+            )
+        ]
+
+    for index in (0, 1):
+        whole(index)
+        for step in range(1, 8):
+            for copy in pieces(index, step, me, (me + step) % 8):
+                copy.start()
+        for copy in own_pieces(index):
+            copy.start()
+
+    fulls = (one_full, two_full, mix_full, narrow_full)
+
+    def spot(index, quarter):
+        count = fulls[index].shape[0] // 4
+        return fulls[index].at[pl.ds(pl.multiple_of(quarter * count, count), count), :]
+
+    def hand(index, lane, source, quarter, device):
+        return remote(
+            source, spot(index, quarter), fs.at[index, lane], fr.at[index, lane], device
+        )
+
+    own_full = []
+    for index in (2, 3):
+        whole(index)
+        source = grads[index][1].at[1]
+        hand(index, 0, source, rep, (across, me)).start()
+        hand(index, 1, source, rep, (twin, me)).start()
+        copy = pltpu.make_async_copy(source, spot(index, rep), ds_sem.at[3 + index])
+        copy.start()
+        own_full.append(copy)
+
+    for index in (0, 1):
+        for copy in own_pieces(index):
+            copy.wait()
+        for step in range(1, 8):
+            source_shard = (me + 8 - step) % 8
+            for copy in pieces(index, step, source_shard, me):
+                copy.wait_recv()
+        hand(index, 0, spot(index, rep), rep, (across, me)).start()
+        hand(index, 1, spot(index, rep), rep, (twin, me)).start()
+
+    for index in (0, 1):
+        col_copy(index, 0).wait_recv()
+        act_load(index, 0).wait()
+        for step in range(1, 4):
+            line_copy(index, step).wait_recv()
+
+        def body(rows, index=index):
+            value = loc_act[index, 0, rows, :].astype(jnp.float32)
+            value = value + col_act[index, 0, rows, :].astype(jnp.float32)
+            for step in range(3):
+                value = value + line_act[index, step, rows, :].astype(jnp.float32)
+            total[index, rows, :] = value
+
+        rows_loop(total.shape[1], 16, body)
+    outs = [
+        pltpu.make_async_copy(total.at[0], out_sum, ds_sem.at[7]),
+        pltpu.make_async_copy(total.at[1], in_sum, ds_sem.at[8]),
+    ]
+    for copy in outs:
+        copy.start()
+
+    for step in range(1, 4):
+        vec_share(step).wait_recv()
+    vec_full[...] = vec_mid[...] + vec_rep[0] + vec_rep[1] + vec_rep[2]
+
+    for index in (2, 3, 0, 1):
+        hand(index, 0, spot(index, across), across, (across, me)).wait_recv()
+        hand(index, 2, spot(index, across), across, (twin, me)).start()
+    for index in range(4):
+        source = grads[index][1].at[1] if index > 1 else spot(index, rep)
+        hand(index, 0, source, rep, (across, me)).wait_send()
+        hand(index, 1, source, rep, (twin, me)).wait_send()
+        hand(index, 1, spot(index, twin), twin, (twin, me)).wait_recv()
+        hand(index, 2, spot(index, across), across, (twin, me)).wait_send()
+        hand(index, 2, spot(index, diagonal), diagonal, (twin, me)).wait_recv()
+        side_copy(index).wait_send()
+        for slot in (0, 1):
+            core_copy(index, slot).wait_send()
+    for index in (0, 1):
+        for step in range(1, 8):
+            for copy in pieces(index, step, me, (me + step) % 8):
+                copy.wait_send()
+        for step in range(4):
+            col_copy(index, step).wait_send()
+            if step:
+                line_copy(index, step).wait_send()
+    for step in range(1, 8):
+        vec_copy(step).wait_send()
+    for step in range(1, 4):
+        vec_share(step).wait_send()
+    for copy in own_full + outs:
+        copy.wait()
+
+
+def gather_sums(out_part, in_part, one, two, mix, narrow, vec):
+    dma = pltpu.SemaphoreType.DMA
+    bf16, f32 = jnp.bfloat16, jnp.float32
+    _, length, width = out_part.shape
+    shards, _, share, one_wide = one.shape
+    two_wide = two.shape[3]
+    struct = jax.ShapeDtypeStruct
+    grads = [(g.shape[0],) + g.shape[2:] for g in (one, two)]
+    grads += [g.shape[1:] for g in (mix, narrow)]
+    return pl.pallas_call(
+        gather_sums_kernel,
+        out_shape=(
+            struct((length, width), f32),
+            struct((length, width), f32),
+            struct((4 * share, shards * one_wide), bf16),
+            struct((4 * share, shards * two_wide), bf16),
+            struct((4 * mix.shape[1], width), bf16),
+            struct((4 * narrow.shape[1], width), bf16),
+            struct(vec.shape[1:], f32),
+        ),
+        in_specs=[ANY] * 7,
+        out_specs=(ANY,) * 6 + (pl.BlockSpec(memory_space=pltpu.VMEM),),
+        scratch_shapes=[pltpu.VMEM((2,) + g, bf16) for g in grads]
+        + [pltpu.VMEM((2,) + g, bf16) for g in grads]
+        + [pltpu.VMEM(g, bf16) for g in grads]
+        + [
+            pltpu.VMEM((2, 4, length, width), bf16),
+            pltpu.VMEM((2, 4, length, width), bf16),
+            pltpu.VMEM((2, 3, length, width), bf16),
+            pltpu.VMEM((2, length, width), f32),
+            pltpu.VMEM(vec.shape[1:], f32),
+            pltpu.VMEM((7,) + vec.shape[1:], f32),
+            pltpu.VMEM(vec.shape[1:], f32),
+            pltpu.VMEM((3,) + vec.shape[1:], f32),
+            dma((6, 4)),
+            dma((4, 2)), dma((4, 2)), dma((4,)), dma((4,)),
+            dma((2, 4)), dma((2, 4)), dma((2, 3)), dma((2, 3)),
+            dma((8, 4)), dma((8, 4)), dma((4, 3)), dma((4, 3)),
+            dma((7,)), dma((7,)), dma((3,)), dma((3,)), dma((9,)),
+        ],
+        compiler_params=pltpu.CompilerParams(
+            collective_id=1, has_side_effects=True, vmem_limit_bytes=56 << 20
+        ),
+        name="gather_sums",
+    )(out_part, in_part, one, two, mix, narrow, vec)
+
+
+def turn(values, cosine, sine, sign):
+    half = ROT // 2
+    front, back = values[..., :half], values[..., half:ROT]
+    return jnp.concatenate(
+        [
+            front * cosine - sign * back * sine,
+            back * cosine + sign * front * sine,
+            values[..., ROT:],
+        ],
+        axis=-1,
+    )
+
+
+def matmul(left, right):
+    return jnp.dot(left, right, preferred_element_type=jnp.float32)
+
+
+def tensor_parallel(
+    tokens,
+    segment_ids,
+    positions,
+    first_gain,
+    first_shift,
+    project_weight,
+    project_bias,
+    mixing_weight,
+    mixing_bias,
+    second_gain,
+    second_shift,
+    widen_weight,
+    widen_bias,
+    narrow_weight,
+    narrow_bias,
+    cotangent,
+):
+    f32, bf16 = jnp.float32, jnp.bfloat16
+    length = tokens.shape[0]
+    me = lax.axis_index("shard")
+    packed = jnp.concatenate(
+        [
+            first_gain, first_shift, second_gain, second_shift, mixing_bias, narrow_bias,
+            project_bias, widen_bias, segment_ids.astype(f32), positions.astype(f32),
+            jnp.zeros((512,), f32),
+        ]
+    ).reshape(32, 128)
+    tok_all, cot_all, cols_one, cols_two, small = spread(
+        tokens, cotangent, project_weight, widen_weight, packed
+    )
+
+    def param(start, rows):
+        return small[:, start : start + rows].reshape(-1)
+
+    gain_one, shift_one, gain_two, shift_two = (param(2 * i, 2) for i in range(4))
+    out_bias = param(8, 2) + param(10, 2)
+    head_bias = lax.dynamic_index_in_dim(
+        param(12, 6).reshape(3, HEADS, HEAD_DIM), me, 1, keepdims=False
+    ).reshape(-1)
+    segments = small[:, 26]
+    places_all = small[:, 27]
+
+    inputs = tok_all.reshape(-1, D).astype(f32)
+    center = inputs - jnp.mean(inputs, axis=-1, keepdims=True)
+    scale = lax.rsqrt(jnp.mean(center * center, axis=-1, keepdims=True) + 1e-05)
+    norm = center * scale
+    first = (norm * gain_one + shift_one).astype(bf16)
+    second = (norm * gain_two + shift_two).astype(bf16)
+    cot = cot_all.reshape(-1, D)
+
+    widened = matmul(second, cols_two) + widen_bias
+    cdf = 0.5 * (1.0 + lax.erf(widened * (0.5**0.5)))
+    density = jnp.exp(-0.5 * widened * widened) * (1.0 / (2.0 * jnp.pi) ** 0.5)
+    active = (widened * cdf).astype(bf16)
+    slope = cdf + widened * density
+    d_widened = (times_rows(cot, narrow_weight) * slope).astype(bf16)
+
+    joint = matmul(first, cols_one) + head_bias
+    cosine, sine = angles(places_all.reshape(-1))
+    raw_q, raw_k, raw_v = (
+        joint[:, i * HEAD_DIM : (i + 1) * HEAD_DIM] for i in range(3)
+    )
+    shape = (8, length, HEAD_DIM)
+    query = (turn(raw_q, cosine, sine, 1.0) * HEAD_DIM**-0.5).astype(bf16).reshape(shape)
+    keys = turn(raw_k, cosine, sine, 1.0).astype(bf16).reshape(shape)
+    values = raw_v.astype(bf16).reshape(shape)
+    order = jnp.arange(length)
+    allowed = (segments[:, :, None] == segments[:, None, :]) & (
+        order[:, None] >= order[None, :]
+    )
+
+    def batched(left, right, dims):
+        return lax.dot_general(
+            left, right, (dims, ((0,), (0,))), preferred_element_type=f32
+        )
+
+    scores = jnp.where(allowed, batched(query, keys, ((2,), (2,))), -1e30)
+    highest = jnp.max(scores, axis=-1, keepdims=True)
+    lifted = jnp.exp(scores - highest)
+    probs = lifted / jnp.sum(lifted, axis=-1, keepdims=True)
+    probs_low = probs.astype(bf16)
+    context = batched(probs_low, values, ((2,), (1,))).astype(bf16)
+    d_context = times_rows(cot, mixing_weight).astype(bf16).reshape(shape)
+    d_probs = batched(d_context, values, ((2,), (2,)))
+    d_values = batched(probs_low, d_context, ((1,), (1,)))
+    d_scores = (
+        probs * (d_probs - jnp.sum(d_probs * probs, axis=-1, keepdims=True))
+    ).astype(bf16)
+    d_query = batched(d_scores, keys, ((2,), (1,))).reshape(-1, HEAD_DIM)
+    d_keys = batched(d_scores, query, ((1,), (1,))).reshape(-1, HEAD_DIM)
+    d_joint = jnp.concatenate(
+        [
+            turn(d_query, cosine, sine, -1.0) * HEAD_DIM**-0.5,
+            turn(d_keys, cosine, sine, -1.0),
+            d_values.reshape(-1, HEAD_DIM),
+        ],
+        axis=1,
+    ).astype(bf16)
+    context = context.reshape(-1, HEAD_DIM)
+
+    out_part = (matmul(context, mixing_weight) + matmul(active, narrow_weight)).astype(bf16)
+    out_part = out_part.reshape(8, length, D)
+    d_first = times_rows(d_joint, cols_one)
+    d_second = times_rows(d_widened, cols_two)
+    in_part = (d_first * gain_one + d_second * gain_two).astype(bf16)
+    in_part = in_part.reshape(8, length, D)
+
+    def quarters(array):
+        return array.reshape(8, 4, -1, array.shape[1])
+
+    grad_one = quarters(contract_rows(first, d_joint).astype(bf16))
+    grad_two = quarters(contract_rows(second, d_widened).astype(bf16))
+    grad_mix = contract_rows(context, cot).astype(bf16).reshape(4, -1, D)
+    grad_narrow = contract_rows(active, cot).astype(bf16).reshape(4, -1, D)
+
+    def at_own(array, count):
+        zeros = jnp.zeros((8, count), f32)
+        return lax.dynamic_update_slice(zeros, array.reshape(1, count), (me, 0))
+
+    head_sums = jnp.sum(d_joint, axis=0, dtype=f32).reshape(3, 1, HEAD_DIM)
+    head_sums = lax.dynamic_update_slice(
+        jnp.zeros((3, HEADS, HEAD_DIM), f32), head_sums, (0, me, 0)
+    )
+    vec = jnp.concatenate(
+        [
+            jnp.sum(d_first * norm, axis=0).reshape(8, -1),
+            jnp.sum(d_first, axis=0).reshape(8, -1),
+            jnp.sum(d_second * norm, axis=0).reshape(8, -1),
+            jnp.sum(d_second, axis=0).reshape(8, -1),
+            head_sums.reshape(8, -1),
+            jnp.sum(cotangent, axis=0, dtype=f32).reshape(8, -1),
+            at_own(jnp.sum(d_widened, axis=0, dtype=f32), FF // 8),
+        ],
+        axis=1,
+    ).reshape(8, 24, 128)
+
+    out_sum, in_sum, full_one, full_two, full_mix, full_narrow, sums = gather_sums(
+        out_part, in_part, grad_one, grad_two, grad_mix, grad_narrow, vec
+    )
+    own = tokens.astype(f32)
+    own_center = own - jnp.mean(own, axis=-1, keepdims=True)
+    own_scale = lax.rsqrt(
+        jnp.mean(own_center * own_center, axis=-1, keepdims=True) + 1e-05
+    )
+    own_norm = own_center * own_scale
+    output = (own + out_sum + out_bias).astype(bf16)
+    pulled = own_scale * (
+        in_sum
+        - jnp.mean(in_sum, axis=-1, keepdims=True)
+        - own_norm * jnp.mean(in_sum * own_norm, axis=-1, keepdims=True)
+    )
+    input_grad = (cotangent.astype(f32) + pulled).astype(bf16)
+    flat = sums.reshape(-1)
+    return (
+        output,
+        input_grad,
+        flat[:256],
+        flat[256:512],
+        full_one.astype(f32),
+        flat[1024:1792],
+        full_mix.astype(f32),
+        flat[1792:2048],
+        flat[512:768],
+        flat[768:1024],
+        full_two.astype(f32),
+        flat[2048:3072],
+        full_narrow.astype(f32),
+        flat[1792:2048],
+    )
+
+
 def solution(mesh):
+    head_per_shard = mesh.shape["shard"] == HEADS and mesh.shape["rep"] == 4
+    chosen = tensor_parallel if head_per_shard else per_device
     in_specs = (
         P(("rep", "shard"), None),
         P(("rep", "shard")),
@@ -280,5 +1140,5 @@
         P("shard"),
     )
     return jax.shard_map(
-        per_device, mesh=mesh, in_specs=in_specs, out_specs=out_specs, check_vma=False
-    )
+        chosen, mesh=mesh, in_specs=in_specs, out_specs=out_specs, check_vma=False
+    )

time: 3890 us -> 485 us (0.12)
  waiting for transfers between devices: 3400 us -> 0 us
  Pallas kernels: 0 us -> 318 us
  blocking collectives: 191 us -> 0 us
  matrix products: 166 us -> 85.5 us
    all_gather x4 -> x0, waiting for transfers between devices: 1650 us -> none  [the longest x1 622 us: per_device(): lax.all_gather(narrow_weight, 'shard', axis=0, tiled=True)]
    reduce_scatter x2 -> x0, waiting for transfers between devices: 1450 us -> none  [the longest x1 1060 us: per_device(): lax.psum_scatter(wide_term(jnp.int32(0), lax.axis_size('shard') * (D // s...]
    pallas_call x0 -> x2, Pallas kernels: none -> 318 us  [the longest x1 182 us: gather_sums(): pl.pallas_call(gather_sums_kernel, out_shape=(struct((length, width), f32...]
    psum x2 -> x0, waiting for transfers between devices: 301 us -> none  [the longest x1 217 us: per_device(): lax.psum(wide_part.astype(jnp.bfloat16), 'rep').astype(jnp.float32)]
    all_gather x8 -> x0, blocking collectives: 191 us -> none  [the longest x1 55.4 us: per_device(): lax.all_gather(second_gain, 'shard', axis=0, tiled=True)]
    concatenate x1 -> x0, other arithmetic: 44.6 us -> none  [wide_term(): jnp.concatenate([contract_rows(left_one, d_joint), contract_rows(left_two...]
  transfers between devices with their start and end apart: 8 -> 0, of which waited for: 8 -> 0; matrix products, arithmetic and copies ran while one was open for 7% -> 0% of each run, Pallas kernels for 0% -> 0%
where the time goes in v1:
time: 485 us; the launch traced here: 479 us
  Pallas kernels  318 us (66%)
  matrix products  85.5 us (18%)
  other arithmetic  41.4 us (9%)
  local copies, waits for them, and re-layouts  33.3 us (7%)
    pallas_call x1, Pallas kernels, gather_sums(): pl.pallas_call(gather_sums_kernel, out_shape=(struct((length, width), f32...  182 us
    pallas_call x1, Pallas kernels, spread(): pl.pallas_call(spread_kernel, out_shape=(jax.ShapeDtypeStruct((8, length,...  136 us
    dot_general x4, matrix products, times_rows(): lax.dot_general(left, piece, (((1,), (1,)), ((), ())), preferred_element_...  28.1 us
    dot_general x4, matrix products, contract_rows(): lax.dot_general(left, right, (((0,), (0,)), ((), ())), preferred_element_...  25.4 us
    dot_general x4, matrix products, matmul(): return jnp.dot(left, right, preferred_element_type=jnp.float32)  21.8 us
    unnamed x119, local copies, waits for them, and re-layouts  18.6 us
    dot_general x6, matrix products, batched(): lax.dot_general(left, right, (dims, ((0,), (0,))), preferred_element_type...  10.2 us

profile of v1, /device:TPU:29, one launch (start us, length us, event | category | flops | bytes accessed | tf_op | source)
XLA Modules:
  0.0 479.3 jit_solution(1461148919058300149)
XLA Ops:
  0.7 1.3 convert_reduce_fusion.3
  2.0 1.3 fusion.18
  3.8 1.1 convert_reduce_fusion.4
  6.2 0.7 constant_dynamic-update-slice_fusion
  6.9 0.7 constant_dynamic-update-slice_fusion.10
  7.6 0.7 constant_dynamic-update-slice_fusion.9
  8.2 0.7 constant_dynamic-update-slice_fusion.12
  8.9 0.7 constant_dynamic-update-slice_fusion.11
  9.6 0.7 constant_dynamic-update-slice_fusion.18
  10.3 0.7 constant_dynamic-update-slice_fusion.17
  11.0 0.7 constant_dynamic-update-slice_fusion.16
  11.7 0.7 constant_dynamic-update-slice_fusion.15
  12.3 0.7 constant_dynamic-update-slice_fusion.14
  13.6 135.7 %spread.1 = (bf16[8,128,2048]{2,1,0:T(8,128)(2,1)}, bf16[8,128,2048]{2,1,0:T(8,128)(2,1)}, bf16[2048,768]{1,0:T(8,128)(2,1)}, bf16[2048,1024]{1,0:T(8,128)(2,1)}, f32[8,32,128]{2,1,0:T(8,128)}) custom-call(bf16[128,2048]{1,0:T(8,128)(2,1)} %tok.1, bf16[128,2048]{1,0:T(8,128)(2,1)} %cot.1, bf16[256,6144]{1,0:T(8,128)(2,1)} %wide_one.1, ...), custom_call_target="tpu_custom_call" | custom-call | tf_op jit(solution)/shard_map/spread/pallas_call | solution.py:535
  149.3 3.0 convert_reduce_fusion
  152.7 1.2 multiply_reduce_fusion.2
  154.7 4.4 convolution_convert_fusion.5
  159.2 4.5 add_convert_fusion.3
  163.7 5.3 %fusion.65 = (bf16[1024,768]{0,1:T(8,128)(2,1)S(1)}, f32[1024,768]{0,1:T(8,128)}) fusion(f32[768]{0:T(1024)S(1)} %add.124, bf16[1024,2048]{1,0:T(8,128)(2,1)S(1)} %get-tuple-element.47, bf16[2048,768]{1,0:T(8,128)(2,1)S(1)} %copy-done.44), kind=kOutput, calls=%fused_computation.139 | convolution fusion | flops 3222798336 | bytes 12061696 | tf_op jit(solution)/shard_map/dot_general | solution.py:930
  169.1 1.0 copy.70
  170.1 1.0 copy.66
  171.1 1.7 fusion.44
  172.8 1.2 slice.158
  173.9 0.8 copy.64
  174.8 0.8 copy.65
  177.0 0.8 copy-done.18
  177.9 1.8 convolution_select_fusion
  179.7 0.7 fusion.66
  180.5 2.6 convolution_convert_fusion.4
  183.1 2.5 convolution_convert_fusion.3
  185.6 1.3 multiply_reduce_fusion.3
  187.7 2.1 copy.69
  189.8 1.3 fusion.68
  191.1 1.0 slice.168
  192.1 2.0 copy.76
  194.1 1.1 fusion.62
  195.2 1.2 copy.74
  196.4 1.9 copy.75
  198.6 1.2 copy.73
  199.8 1.1 fusion.63
  200.9 1.2 copy.71
  202.1 1.2 copy.72
  203.4 1.4 fusion.47
  204.8 1.5 fusion.56
  206.3 1.5 fusion.55
  207.8 1.0 convert_dynamic-update-slice_fusion
  208.9 4.9 %convolution_convert_fusion.2 = bf16[2048,768]{1,0:T(8,128)(2,1)} fusion(bf16[1024,2048]{1,0:T(8,128)(2,1)S(1)} %copy-done.12, bf16[1024,768]{0,1:T(8,128)(2,1)S(1)} %constant_dynamic-update-slice_fusion.1), kind=kOutput, calls=%fused_computation.23 | convolution fusion | flops 3222798336 | bytes 8912896 | tf_op jit(solution)/shard_map/dot_general | solution.py:41
  214.2 4.6 fusion.8
  218.8 6.2 %fusion.69 = f32[1024,2048]{1,0:T(8,128)} fusion(bf16[1024,768]{0,1:T(8,128)(2,1)S(1)} %copy-done.17, bf16[2048,768]{1,0:T(8,128)(2,1)S(1)} %copy-done.45), kind=kOutput, calls=%fused_computation.143 | convolution fusion | flops 3221225472 | bytes 13107200 | tf_op jit(solution)/shard_map/dot_general | solution.py:47
  225.1 6.2 %multiply_convert_fusion = (bf16[1024,1024]{1,0:T(8,128)(2,1)}, f32[1024,1024]{1,0:T(8,128)S(1)}) fusion(f32[1024]{0:T(1024)S(1)} %copy-done.40, bf16[1024,2048]{1,0:T(8,128)(2,1)S(1)} %copy-done.10, bf16[2048,1024]{1,0:T(8,128)(2,1)S(1)} %copy-done.43), kind=kOutput, calls=%fused_computation.19 | convolution fusion | flops 4301258752 | bytes 14684160 | tf_op jit(solution)/shard_map/dot_general | solution.py:930
  231.3 6.1 %convert_reduce_fusion.1 = (f32[1024]{0:T(1024)S(1)}, bf16[1024,1024]{1,0:T(8,128)(2,1)S(1)}) fusion(f32[1024,1024]{1,0:T(8,128)S(1)} %get-tuple-element.76, f32[1024]{0:T(1024)S(1)} %copy-done.40, bf16[1024,2048]{1,0:T(8,128)(2,1)S(1)} %bitcast.103, bf16[1024,2048]{1,0:T(8,128)(2,1)S(1)} %copy-done.42), kind=kOutput, calls=%fused_computation.18 | convolution fusion | flops 4308597760 | bytes 14688256 | tf_op jit(solution)/shard_map/dot_general | solution.py:47
  237.5 11.3 %fusion.59 = (f32[2048]{0:T(1024)S(1)}, f32[2048]{0:T(1024)S(1)}, bf16[1024,2048]{1,0:T(8,128)(2,1)}, f32[2048]{0:T(1024)S(1)}, f32[2048]{0:T(1024)S(1)}) fusion(f32[1024]{0:T(1024)S(1)} %copy-done.34, f32[1024]{0:T(1024)S(1)} %get-tuple-element.73, bf16[8,128,2048]{2,1,0:T(8,128)(2,1)S(1)} %copy-done.3, f32[2048]{0:T(1024)S(1)} %bitcast.135, ...), kind=kOutput, calls=%fused_computation.133 | convolution fusion | flops 4322222080 | bytes 23126016 | tf_op jit(solution)/shard_map/dot_general | solution.py:47
  249.1 9.6 %convolution_convert_fusion.1 = bf16[2048,1024]{1,0:T(8,128)(2,1)} fusion(bf16[1024,2048]{1,0:T(8,128)(2,1)} %get-tuple-element.48, bf16[1024,1024]{1,0:T(8,128)(2,1)} %copy-done.47), kind=kOutput, calls=%fused_computation.22 | convolution fusion | flops 4297064448 | bytes 10485760 | tf_op jit(solution)/shard_map/dot_general | solution.py:41
  258.7 6.3 %convolution_convert_fusion = bf16[1024,2048]{1,0:T(8,128)(2,1)} fusion(bf16[1024,1024]{1,0:T(8,128)(2,1)S(1)} %copy-done.46, bf16[1024,2048]{1,0:T(8,128)(2,1)S(1)} %bitcast.104), kind=kOutput, calls=%fused_computation.21 | convolution fusion | flops 4297064448 | bytes 10485760 | tf_op jit(solution)/shard_map/dot_general | solution.py:41
  265.1 0.7 copy.79
  265.8 6.9 %fusion.67 = f32[1024,2048]{1,0:T(8,128)S(1)} fusion(bf16[1024,1024]{1,0:T(8,128)(2,1)} %get-tuple-element.75, bf16[1024,2048]{1,0:T(8,128)(2,1)} %param.29), kind=kOutput, calls=%fused_computation.141 | convolution fusion | flops 4294967296 | bytes 14680064 | tf_op jit(solution)/shard_map/dot_general | solution.py:930
  272.7 3.4 add_convert_fusion.1
  276.1 182.0 %gather_sums.1 = (f32[128,2048]{1,0:T(8,128)}, f32[128,2048]{1,0:T(8,128)}, bf16[256,6144]{1,0:T(8,128)(2,1)}, bf16[256,8192]{1,0:T(8,128)(2,1)}, bf16[256,2048]...) custom-call(bf16[8,128,2048]{2,1,0:T(8,128)(2,1)} %bitcast.101, bf16[8,128,2048]{2,1,0:T(8,128)(2,1)} %bitcast.109, ...), custom_call_target="tpu_custom_call" | custom-call | tf_op jit(solution)/shard_map/gather_sums/pallas_call | solution.py:878
  458.1 1.7 fusion.61
  459.9 3.1 fusion.19
  464.7 1.5 convert_element_type.124
  466.3 3.4 convert_element_type.123
  469.7 4.4 convert_element_type.125
  474.1 4.4 convert_element_type.126
  (144 shorter events, 9.4 us)
Async XLA Ops:
  0.6 154.1 %copy-start = (bf16[256,2048]{1,0:T(8,128)(2,1)S(1)}, bf16[256,2048]{1,0:T(8,128)(2,1)}, u32[]{:S(2)}) copy-start(bf16[256,2048]{1,0:T(8,128)(2,1)} %param.23) | copy-start | bytes 3145732
  0.7 170.4 %copy-start.36 = (f32[32]{0:T(128)}, f32[32]{0:T(128)S(1)}, u32[]{:S(2)}) copy-start(f32[32]{0:T(128)S(1)} %negate_power_fusion) | copy-start | bytes 388
  2.0 1.3 copy-start.37
  13.0 0.6 copy-start.32
  149.3 3.5 copy-start.1
  149.3 4.7 copy-start.26
  154.0 5.2 %copy-start.33 = (f32[1024]{0:T(1024)}, f32[1024]{0:T(1024)S(1)}, u32[]{:S(2)}) copy-start(f32[1024]{0:T(1024)S(1)} %rsqrt_bitcast_fusion) | copy-start | bytes 12292
  154.6 4.5 copy-start.28
  154.6 4.5 copy-start.30
  154.7 4.5 copy-start.2
  159.2 4.5 copy-start.44
  163.7 5.3 %copy-start.11 = (bf16[1024,2048]{1,0:T(8,128)(2,1)}, bf16[1024,2048]{1,0:T(8,128)(2,1)S(1)}, u32[]{:S(2)}) copy-start(bf16[1024,2048]{1,0:T(8,128)(2,1)S(1)} %get-tuple-element.47) | copy-start | bytes 12582916
  177.0 0.8 copy-start.18
  177.9 7.7 %copy-start.24 = (bf16[1024,256]{1,0:T(8,128)(2,1)S(1)}, bf16[1024,256]{1,0:T(8,128)(2,1)}, u32[]{:S(2)}) copy-start(bf16[1024,256]{1,0:T(8,128)(2,1)} %copy.70) | copy-start | bytes 1572868
  179.7 0.8 copy-start.25
  180.5 6.5 %copy-start.20 = (bf16[1024,192]{1,0:T(8,128)(2,1)S(1)}, bf16[1024,192]{1,0:T(8,128)(2,1)}, u32[]{:S(2)}) copy-start(bf16[1024,192]{1,0:T(8,128)(2,1)} %copy.66) | copy-start | bytes 1179652
  180.5 6.5 %copy-start.22 = (bf16[1024,32]{1,0:T(8,128)(2,1)S(1)}, bf16[1024,32]{1,0:T(8,128)(2,1)}, u32[]{:S(2)}) copy-start(bf16[1024,32]{1,0:T(8,128)(2,1)} %copy.64) | copy-start | bytes 196612
  180.5 6.6 %copy-start.23 = (bf16[1024,32]{1,0:T(8,128)(2,1)S(1)}, bf16[1024,32]{1,0:T(8,128)(2,1)}, u32[]{:S(2)}) copy-start(bf16[1024,32]{1,0:T(8,128)(2,1)} %copy.65) | copy-start | bytes 196612
  199.8 4.9 %copy-start.14 = (f32[1024,192]{0,1:T(8,128)S(1)}, f32[1024,192]{0,1:T(8,128)}, u32[]{:S(2)}) copy-start(f32[1024,192]{0,1:T(8,128)} %copy.73) | copy-start | bytes 2359300
  199.8 9.0 %copy-start.19 = (bf16[1024,256]{0,1:T(8,128)(2,1)S(1)}, bf16[1024,256]{0,1:T(8,128)(2,1)}, u32[]{:S(2)}) copy-start(bf16[1024,256]{0,1:T(8,128)(2,1)} %copy.69) | copy-start | bytes 1572868
  203.4 5.5 %copy-start.12 = (bf16[1024,2048]{1,0:T(8,128)(2,1)S(1)}, bf16[1024,2048]{1,0:T(8,128)(2,1)}, u32[]{:S(2)}) copy-start(bf16[1024,2048]{1,0:T(8,128)(2,1)} %copy-done.11) | copy-start | bytes 12582916
  208.9 5.0 %copy-start.16 = (bf16[1024,768]{0,1:T(8,128)(2,1)}, bf16[1024,768]{0,1:T(8,128)(2,1)S(1)}, u32[]{:S(2)}) copy-start(bf16[1024,768]{0,1:T(8,128)(2,1)S(1)} %constant_dynamic-update-slice_fusion.1) | copy-start | bytes 4718596
  208.9 5.3 %copy-start.13 = (bf16[8,128,256]{2,1,0:T(8,128)(2,1)S(1)}, bf16[8,128,256]{2,1,0:T(8,128)(2,1)}, u32[]{:S(2)}) copy-start(bf16[8,128,256]{2,1,0:T(8,128)(2,1)} %convolution_convert_fusion.4) | copy-start | bytes 1572868
  214.2 4.6 copy-start.17
  214.2 4.6 copy-start.45
  218.8 6.2 %copy-start.10 = (bf16[1024,2048]{1,0:T(8,128)(2,1)S(1)}, bf16[1024,2048]{1,0:T(8,128)(2,1)}, u32[]{:S(2)}) copy-start(bf16[1024,2048]{1,0:T(8,128)(2,1)} %get-tuple-element.48) | copy-start | bytes 12582916
  218.8 6.2 %copy-start.40 = (f32[1024]{0:T(1024)S(1)}, f32[1024]{0:T(1024)}, u32[]{:S(2)}) copy-start(f32[1024]{0:T(1024)} %param.28) | copy-start | bytes 12292
  218.8 6.2 %copy-start.43 = (bf16[2048,1024]{1,0:T(8,128)(2,1)S(1)}, bf16[2048,1024]{1,0:T(8,128)(2,1)}, u32[]{:S(2)}) copy-start(bf16[2048,1024]{1,0:T(8,128)(2,1)} %get-tuple-element.29) | copy-start | bytes 12582916
  225.1 6.2 %copy-start.5 = (bf16[8,128,2048]{2,1,0:T(8,128)(2,1)S(1)}, bf16[8,128,2048]{2,1,0:T(8,128)(2,1)}, u32[]{:S(2)}) copy-start(bf16[8,128,2048]{2,1,0:T(8,128)(2,1)} %get-tuple-element.30) | copy-start | bytes 12582916
  225.1 6.2 %copy-start.42 = (bf16[1024,2048]{1,0:T(8,128)(2,1)S(1)}, bf16[1024,2048]{1,0:T(8,128)(2,1)}, u32[]{:S(2)}) copy-start(bf16[1024,2048]{1,0:T(8,128)(2,1)} %param.29) | copy-start | bytes 12582916
  231.3 6.2 %copy-start.3 = (bf16[8,128,2048]{2,1,0:T(8,128)(2,1)S(1)}, bf16[8,128,2048]{2,1,0:T(8,128)(2,1)}, u32[]{:S(2)}) copy-start(bf16[8,128,2048]{2,1,0:T(8,128)(2,1)} %get-tuple-element.27) | copy-start | bytes 12582916
  231.3 6.2 %copy-start.29 = (f32[8,2,128]{2,1,0:T(2,128)S(1)}, f32[8,2,128]{2,1,0:T(2,128)}, u32[]{:S(2)}) copy-start(f32[8,2,128]{2,1,0:T(2,128)} %copy-done.28) | copy-start | bytes 24580
  231.3 6.2 %copy-start.31 = (f32[8,2,128]{2,1,0:T(2,128)S(1)}, f32[8,2,128]{2,1,0:T(2,128)}, u32[]{:S(2)}) copy-start(f32[8,2,128]{2,1,0:T(2,128)} %copy-done.30) | copy-start | bytes 24580
  231.3 6.2 %copy-start.34 = (f32[1024]{0:T(1024)S(1)}, f32[1024]{0:T(1024)}, u32[]{:S(2)}) copy-start(f32[1024]{0:T(1024)} %copy-done.33) | copy-start | bytes 12292
  237.4 11.4 %copy-start.47 = (bf16[1024,1024]{1,0:T(8,128)(2,1)}, bf16[1024,1024]{1,0:T(8,128)(2,1)S(1)}, u32[]{:S(2)}) copy-start(bf16[1024,1024]{1,0:T(8,128)(2,1)S(1)} %get-tuple-element.84) | copy-start | bytes 6291460
  249.1 9.6 %copy-start.6 = (bf16[8,128,2048]{2,1,0:T(8,128)(2,1)S(1)}, bf16[8,128,2048]{2,1,0:T(8,128)(2,1)}, u32[]{:S(2)}) copy-start(bf16[8,128,2048]{2,1,0:T(8,128)(2,1)} %get-tuple-element.30) | copy-start | bytes 12582916
  249.1 9.6 %copy-start.46 = (bf16[1024,1024]{1,0:T(8,128)(2,1)S(1)}, bf16[1024,1024]{1,0:T(8,128)(2,1)}, u32[]{:S(2)}) copy-start(bf16[1024,1024]{1,0:T(8,128)(2,1)} %get-tuple-element.75) | copy-start | bytes 6291460
  258.7 6.4 %copy-start.27 = (f32[8,256]{1,0:T(8,128)S(1)}, f32[8,256]{1,0:T(8,128)}, u32[]{:S(2)}) copy-start(f32[8,256]{1,0:T(8,128)} %reshape.234) | copy-start | bytes 24580
  276.1 182.0 %copy-start.4 = (bf16[128,2048]{1,0:T(8,128)(2,1)S(1)}, bf16[128,2048]{1,0:T(8,128)(2,1)}, u32[]{:S(2)}) copy-start(bf16[128,2048]{1,0:T(8,128)(2,1)} %tok.1) | copy-start | bytes 1572868
  276.1 182.0 %copy-start.38 = (f32[128]{0:T(128)S(1)}, f32[128]{0:T(128)}, u32[]{:S(2)}) copy-start(f32[128]{0:T(128)} %copy-done.37) | copy-start | bytes 1540
  276.1 182.0 %copy-start.41 = (f32[128]{0:T(128)S(1)}, f32[128]{0:T(128)}, u32[]{:S(2)}) copy-start(f32[128]{0:T(128)} %add_rsqrt_fusion) | copy-start | bytes 1540
  276.1 183.8 %copy-start.7 = (bf16[128,2048]{1,0:T(8,128)(2,1)S(1)}, bf16[128,2048]{1,0:T(8,128)(2,1)}, u32[]{:S(2)}) copy-start(bf16[128,2048]{1,0:T(8,128)(2,1)} %cot.1) | copy-start | bytes 1572868
  458.1 4.9 %copy-start.35 = (f32[24,128]{1,0:T(8,128)S(1)}, f32[24,128]{1,0:T(8,128)}, u32[]{:S(2)}) copy-start(f32[24,128]{1,0:T(8,128)} %get-tuple-element.33) | copy-start | bytes 36868
  458.1 6.6 %copy-start.21 = (bf16[256,2048]{1,0:T(8,128)(2,1)S(1)}, bf16[256,2048]{1,0:T(8,128)(2,1)}, u32[]{:S(2)}) copy-start(bf16[256,2048]{1,0:T(8,128)(2,1)} %get-tuple-element.35) | copy-start | bytes 3145732
  458.1 8.1 %copy-start.15 = (bf16[256,6144]{1,0:T(8,128)(2,1)S(1)}, bf16[256,6144]{1,0:T(8,128)(2,1)}, u32[]{:S(2)}) copy-start(bf16[256,6144]{1,0:T(8,128)(2,1)} %get-tuple-element.34) | copy-start | bytes 9437188
  464.7 13.8 %copy-start.39 = (f32[256]{0:T(256)}, f32[256]{0:T(256)S(1)}, u32[]{:S(2)}) copy-start(f32[256]{0:T(256)S(1)} %get-tuple-element.114) | copy-start | bytes 3076
  466.3 3.5 copy-start.9
  469.7 4.4 copy-start.8
